TPU v7x, 256 devices: a whole 4x4x8 slice. The times are simulated.
256 devices in a mesh: clip: 16 (over z, core), row: 4 (over y), tm: 4 (over x).
Axes of the slice: x: 4, y: 4, z: 8, core: 2. Of those that a mesh axis runs over, the one named last changes fastest.
Arguments:
- frames: bfloat16 [128, 3, 16, 1024], P('clip', None, 'tm', 'row'), may hold values from -6 to 6
- keep_list: int32 [128], P('clip'), may hold values from -1 to 63, as said below
- train_slot: int32 [64], replicated, may hold values from 0 to 63, as said below
- stem_weight: bfloat16 [81, 128], replicated, may hold values from -0.625 to 0.625
- stem_gain: float32 [128], replicated, may hold values from 0.1 to 1.9
- stem_shift: float32 [128], replicated, may hold values from -3 to 3
- mixer_weight: bfloat16 [3, 3, 384, 256], replicated, may hold values from -0.109375 to 0.109375
- mixer_gain: float32 [256], replicated, may hold values from 0.1 to 1.9
- mixer_shift: float32 [256], replicated, may hold values from -3 to 3
- down_weight: bfloat16 [1024, 256], replicated, may hold values from -0.1875 to 0.1875
- down_bias: float32 [256], replicated, may hold values from -3 to 3
Outputs:
- latents: bfloat16 [64, 8, 8, 32, 256], P('clip', 'tm', 'row')
Inputs may be any that keep to these rules, and one draw needn't show every extreme that they name: `keep_list`: each encoder position 0 to 63 is named by exactly one slot, and -1 marks a dropped slot; encoder position e belongs to index e // 4 of clip. `train_slot`: A permutation; training position t belongs to index t // 4 of clip; at most 1 encoder positions of one index of clip go to one index of clip.
All inputs are finite; a program needn't handle non-finite values.
Results may differ from a plain program's by a relative error of at most 0.0053.
Values may be sent and summed in bfloat16 or wider, within the bound.
No kernel may reach another device: no remote copies, remote signals or barrier semaphores. Data moves between devices by JAX's collectives and lax.ppermute only.
A program may use at most 64 MiB of HBM per device.

v0:
```python
import jax
import jax.numpy as jnp
from jax import lax
from jax.sharding import PartitionSpec as P

GROUPS = 32
COLS = 64
eps = 1e-06


def from_behind(shard, axis, by):
    size = lax.axis_size(axis)
    pairs = [(i, i + by) for i in range(size) if 0 <= i + by < size]
    return lax.ppermute(shard, axis, pairs)


def extended_2(cells, sides, width):
    for axis, dim in sides:
        count = lax.axis_size(axis)
        ends = count - 1
        head = lax.slice_in_dim(cells, 0, width, axis=dim)
        tail = lax.slice_in_dim(cells, cells.shape[dim] - width, cells.shape[dim], axis=dim)
        cells = jnp.concatenate(
            [
                lax.ppermute(tail, axis, [(i, (i + 1) % count) for i in range(ends)]),
                cells,
                lax.ppermute(head, axis, [((i + 1) % count, i) for i in range(ends)]),
            ],
            axis=dim,
        )
    return cells


def surround_time(volume):
    frame_n = volume.shape[1]
    earlier = from_behind(volume[:, frame_n - 2 :], "tm", 1)
    opening = jnp.broadcast_to(volume[:, :1], earlier.shape)
    earlier = jnp.where(lax.axis_index("tm") == 0, opening, earlier)
    extended = jnp.concatenate([earlier, volume], axis=1)
    extended = extended_2(extended, (("row", 2),), 1)
    return jnp.pad(extended, ((0, 0), (0, 0), (0, 0), (1, 1), (0, 0)))


def norm_silu(hidden, gain, shift):
    batch_n, cell_n, chan_n = hidden.shape
    per_group = chan_n // GROUPS
    value_sum = jnp.sum(hidden, axis=1).reshape(batch_n, GROUPS, per_group).sum(-1)
    square_sum = jnp.sum(hidden * hidden, axis=1).reshape(batch_n, GROUPS, per_group).sum(-1)
    value_sum, square_sum = lax.psum((value_sum, square_sum), ("row", "tm"))
    cell_count = cell_n * per_group * lax.axis_size("row") * lax.axis_size("tm")
    group_mean = value_sum / cell_count
    spread = square_sum / cell_count - group_mean * group_mean
    inverse = lax.rsqrt(spread + eps)
    mean_full = jnp.repeat(group_mean, per_group, axis=1)[:, None, :]
    scale_full = jnp.repeat(inverse, per_group, axis=1)[:, None, :] * gain
    return jax.nn.silu((hidden - mean_full) * scale_full + shift)


def encode(clips, params, col_n, surround):
    (
        stem_weight,
        stem_gain,
        stem_shift,
        mixer_weight,
        mixer_gain,
        mixer_shift,
        down_weight,
        down_bias,
    ) = params
    batch_n, chan_in, frame_n, row_cells = clips.shape
    row_n = row_cells // col_n
    cell_n = frame_n * row_n * col_n
    volume = clips.reshape(batch_n, chan_in, frame_n, row_n, col_n).transpose(0, 2, 3, 4, 1)
    padded = surround(volume)
    tap_views = []
    for time_tap in range(3):
        for row_tap in range(3):
            for col_tap in range(3):
                tap_views.append(
                    padded[
                        :,
                        time_tap : time_tap + frame_n,
                        row_tap : row_tap + row_n,
                        col_tap : col_tap + col_n,
                    ]
                )
    patches = jnp.concatenate(tap_views, axis=-1).reshape(batch_n * cell_n, 27 * chan_in)
    stem = jnp.dot(patches, stem_weight, preferred_element_type=jnp.float32).reshape(
        batch_n, cell_n, -1
    )
    hidden = norm_silu(stem, stem_gain, stem_shift).astype(jnp.bfloat16)
    padded = surround(hidden.reshape(batch_n, frame_n, row_n, col_n, -1))
    accumulated = jnp.zeros((batch_n * cell_n, mixer_weight.shape[3]), jnp.float32)
    for time_tap in range(3):
        for row_tap in range(3):
            tap_strip = jnp.concatenate(
                [
                    padded[
                        :,
                        time_tap : time_tap + frame_n,
                        row_tap : row_tap + row_n,
                        col_tap : col_tap + col_n,
                    ]
                    for col_tap in range(3)
                ],
                axis=-1,
            )
            accumulated = accumulated + jnp.dot(
                tap_strip.reshape(-1, tap_strip.shape[-1]),
                mixer_weight[time_tap, row_tap],
                preferred_element_type=jnp.float32,
            )
    activated = norm_silu(accumulated.reshape(batch_n, cell_n, -1), mixer_gain, mixer_shift).astype(
        jnp.bfloat16
    )
    activated = activated.reshape(batch_n, frame_n, row_n, col_n, -1)
    pooled = (
        (activated[:, 0::2].astype(jnp.float32) + activated[:, 1::2].astype(jnp.float32)) * 0.5
    ).astype(jnp.bfloat16)
    chan_out = pooled.shape[-1]
    blocks = (
        pooled.reshape(batch_n, frame_n // 2, row_n // 2, 2, col_n // 2, 2, chan_out)
        .transpose(0, 1, 2, 4, 3, 5, 6)
        .reshape(-1, 4 * chan_out)
    )
    latent = jnp.dot(blocks, down_weight, preferred_element_type=jnp.float32) + down_bias
    return latent.astype(jnp.bfloat16).reshape(
        batch_n, frame_n // 2, row_n // 2, col_n // 2, chan_out
    )


def encode_layout(clips, params):
    return encode(clips, params, COLS, surround_time)


def select_rows(target, items, slot_n):
    flattened = items.reshape(items.shape[0], -1)
    wanted = jnp.arange(slot_n, dtype=jnp.int32)
    picker = (wanted[:, None] == target[None, :]).astype(jnp.bfloat16)
    return jnp.dot(picker, flattened, preferred_element_type=jnp.float32).astype(jnp.bfloat16)


def combine_sources(received):
    return jnp.sum(received.astype(jnp.float32), axis=0).astype(jnp.bfloat16)


def local(
    frames,
    keep_list,
    train_slot,
    stem_weight,
    stem_gain,
    stem_shift,
    mixer_weight,
    mixer_gain,
    mixer_shift,
    down_weight,
    down_bias,
):
    params = (
        stem_weight,
        stem_gain,
        stem_shift,
        mixer_weight,
        mixer_gain,
        mixer_shift,
        down_weight,
        down_bias,
    )
    group_n = lax.axis_size("clip")
    enc_dev = train_slot.shape[0] // group_n
    slot_n = group_n * enc_dev
    safe_keep = jnp.maximum(keep_list, 0)
    composed = jnp.where(keep_list >= 0, train_slot[safe_keep], -1)
    packed = select_rows(composed, frames, slot_n).reshape((group_n, enc_dev) + frames.shape[1:])
    received = lax.all_to_all(packed, "clip", split_axis=0, concat_axis=0, tiled=True)
    return encode_layout(combine_sources(received), params)


def solution(mesh):
    return jax.shard_map(
        local,
        mesh=mesh,
        in_specs=(
            P("clip", None, "tm", "row"),
            P("clip"),
            P(),
            P(),
            P(),
            P(),
            P(),
            P(),
            P(),
            P(),
            P(),
        ),
        out_specs=P("clip", "tm", "row", None, None),
        check_vma=False,
    )
```

profile of v0, /device:TPU:32, one launch (start us, length us, event | category | flops | bytes accessed | tf_op | source)
XLA Modules:
  0.0 240.4 jit_solution(16834706322915642902)
XLA Ops:
  0.0 0.9 reshape.119
  0.9 0.7 broadcast_maximum_fusion
  1.6 1.3 gather_fusion
  2.9 0.7 compare_select_fusion
  3.8 1.0 reshape.120
  4.8 8.6 %all-to-all-start = ((bf16[16,4,3,4,256]{4,3,2,1,0:T(4,128)(2,1)}), bf16[16,4,3,4,256]{4,3,2,1,0:T(4,128)(2,1)S(1)}, u32[]{:S(2)}, u32[]{:S(2)}) async-start(bf16[16,4,3,4,256]{4,3,2,1,0:T(4,128)(2,1)} %reshape.120), calls=%async_computation | async-start | bytes 786432 | tf_op jit(solution)/shard_map/all_to_all | solution.py:176
  13.4 11.9 %all-to-all-done = bf16[16,4,3,4,256]{4,3,2,1,0:T(4,128)(2,1)S(1)} async-done(((bf16[16,4,3,4,256]{4,3,2,1,0:T(4,128)(2,1)}), bf16[16,4,3,4,256]{4,3,2,1,0:T(4,128)(2,1)S(1)}, u32[]{:S(2)}, u32[]{:S(2)}) %all-to-all-start) | async-done | bytes 393248 | tf_op jit(solution)/shard_map/all_to_all | solution.py:176
  25.6 3.4 %collective-permute-start = (bf16[4,2,4,64,3]{3,2,4,1,0:T(4,128)(2,1)S(1)}, bf16[4,2,4,64,3]{3,2,4,1,0:T(4,128)(2,1)S(1)}, u32[]{:S(2)}, u32[]{:S(2)}) collective-permute-start(bf16[4,2,4,64,3]{3,2,4,1,0:T(4,128)(2,1)S(1)} %slice.325), channel_id=1, source_target_pairs={{0,1},{1,2},{2,3},{4,5},{5,6},{6,7},{8,9},{9,10},{10,11},{12,13},{... | collective-permute-start | bytes 36872 | tf_op jit(solution)/shard_map/ppermute | solution.py:14
  29.0 1.5 collective-permute-done
  30.7 1.3 collective-permute-start.2
  32.0 4.5 %collective-permute-start.1 = (bf16[4,6,1,64,3]{3,2,4,1,0:T(2,128)(2,1)S(1)}, bf16[4,6,1,64,3]{3,2,4,1,0:T(2,128)(2,1)S(1)}, u32[]{:S(2)}, u32[]{:S(2)}) collective-permute-start(bf16[4,6,1,64,3]{3,2,4,1,0:T(2,128)(2,1)S(1)} %get-tuple-element.43), channel_id=1, source_target_pairs={{0,4},{4,8},{8,12},{1,5},{5,9},{9,13},{2,6},{6,10},{10,14},{3,7},{... | collective-permute-start | bytes 27656 | tf_op jit(solution)/shard_map/ppermute | solution.py:25
  36.5 1.6 collective-permute-done.1
  40.5 2.1 copy.36
  42.7 1.7 fusion.49
  44.7 42.5 %all-reduce.3 = (f32[4,32]{1,0:T(4,128)S(1)}, f32[4,32]{1,0:T(4,128)S(1)}) all-reduce(f32[4,32]{1,0:T(4,128)S(1)} %reduce_sum.88, f32[4,32]{1,0:T(4,128)S(1)} %reduce_sum.86), channel_id=1, replica_groups=mesh['clip'=16,'row'=4,'tm'=4] {'row','tm'}, use_global_device_ids=true, to_apply=%region_6.7 | all-reduce | flops 256 | bytes 2048 | tf_op jit(solution)/shard_map/psum | solution.py:49
  87.7 0.6 multiply_convert_fusion.1
  88.4 1.3 collective-permute-start.3
  89.7 6.6 %collective-permute-done.3 = bf16[4,2,4,64,128]{4,3,2,1,0:T(8,128)(2,1)S(1)} collective-permute-done((bf16[4,2,4,64,128]{4,3,2,1,0:T(8,128)(2,1)S(1)}, bf16[4,2,4,64,128]{4,3,2,1,0:T(8,128)(2,1)S(1)}, u32[]{:S(2)}, u32[]{:S(2)}) %collective-permute-start.3) | collective-permute-done | bytes 524320 | tf_op jit(solution)/shard_map/ppermute | solution.py:14
  96.5 1.3 collective-permute-start.5
  97.8 4.8 %collective-permute-start.4 = (bf16[4,6,1,64,128]{4,3,2,1,0:T(8,128)(2,1)S(1)}, bf16[4,6,1,64,128]{4,3,2,1,0:T(8,128)(2,1)S(1)}, u32[]{:S(2)}, u32[]{:S(2)}) collective-permute-start(bf16[4,6,1,64,128]{4,3,2,1,0:T(8,128)(2,1)S(1)} %get-tuple-element.39), channel_id=1, source_target_pairs={{0,4},{4,8},{8,12},{1,5},{5,9},{9,13},{2,6},{6,10},{10,14},{3,7},{... | collective-permute-start | bytes 1179656 | tf_op jit(solution)/shard_map/ppermute | solution.py:25
  102.6 1.1 fusion.16
  103.6 2.6 %collective-permute-done.5 = bf16[4,6,1,64,128]{4,3,2,1,0:T(8,128)(2,1)S(1)} collective-permute-done((bf16[4,6,1,64,128]{4,3,2,1,0:T(8,128)(2,1)S(1)}, bf16[4,6,1,64,128]{4,3,2,1,0:T(8,128)(2,1)S(1)}, u32[]{:S(2)}, u32[]{:S(2)}) %collective-permute-start.5) | collective-permute-done | bytes 393248 | tf_op jit(solution)/shard_map/ppermute | solution.py:27
  106.2 1.5 collective-permute-done.4
  107.6 1.4 select_maximum_fusion
  109.1 6.2 %fusion.50 = (bf16[4,4,4,64,128]{4,3,2,1,0:T(8,128)(2,1)}, bf16[4,4,4,64,128]{4,3,2,1,0:T(8,128)(2,1)}, bf16[4,4,4,64,128]{4,3,2,1,0:T(8,128)(2,1)}, bf16[4,4,4,...) fusion(bf16[4,6,6,66,128]{4,3,2,1,0:T(8,128)(2,1)S(1)} %select_, ...), kind=kLoop, calls=%fused_computation.143 | loop fusion | bytes 37748736 | tf_op jit(solution)/shard_map/slice | solution.py:98
  115.8 0.9 fusion.52
  116.7 1.0 fusion.51
  118.6 1.1 pad_maximum_fusion.1
  120.1 1.2 fusion.28
  121.3 1.2 convolution_add_fusion.7
  122.6 1.1 pad_maximum_fusion.3
  123.6 1.2 convolution_add_fusion.6
  124.9 1.2 convolution_add_fusion.5
  127.0 1.2 convolution_add_fusion.4
  128.2 1.3 pad_maximum_fusion.5
  129.5 1.3 convolution_add_fusion.3
  130.9 1.2 convolution_add_fusion.2
  132.9 0.7 copy-done.9
  133.9 1.3 convolution_add_fusion.1
  135.2 3.2 %bitcast_reduce_fusion = (f32[4,256]{1,0:T(4,128)S(1)}, f32[4,256]{1,0:T(4,128)S(1)}, f32[4096,256]{1,0:T(8,128)}) fusion(f32[4096,256]{1,0:T(8,128)S(1)} %convolution_add_fusion.1, bf16[4096,384]{1,0:T(8,128)(2,1)S(1)} %bitcast.87, bf16[3,3,384,256]{3,2,1,0:T(8,128)(2,1)S(1)} %copy-done.8), kind=kOutput, calls=%fused_computation.14 | convolution fusion | flops 809498624 | bytes 11739136 | tf_op jit(solution)/shard_map/dot_general | solution.py:108
  138.8 38.2 %all-reduce.2 = (f32[4,32]{1,0:T(4,128)S(1)}, f32[4,32]{1,0:T(4,128)S(1)}) all-reduce(f32[4,32]{1,0:T(4,128)S(1)} %reduce_sum.92, f32[4,32]{1,0:T(4,128)S(1)} %reduce_sum.90), channel_id=1, replica_groups=mesh['clip'=16,'row'=4,'tm'=4] {'row','tm'}, use_global_device_ids=true, to_apply=%region_12.13 | all-reduce | flops 256 | bytes 2048 | tf_op jit(solution)/shard_map/psum | solution.py:49
  177.4 6.2 %fusion.4 = bf16[4,4,4,64,256]{4,1,3,2,0:T(4,128)(2,1)S(1)} fusion(f32[4,4,4,64,256]{4,3,2,1,0:T(8,128)} %bitcast.86, f32[256]{0:T(256)S(1)} %copy-done.13, f32[4,256]{1,0:T(4,128)S(1)} %broadcast_multiply_fusion, f32[4,256]{1,0:T(4,128)S(1)} %sub.31), kind=kLoop, calls=%fused_computation.19 | loop fusion | flops 8388608 | bytes 6300672 | tf_op jit(solution)/shard_map/convert_element_type | solution.py:113
  183.6 25.5 %slice.321 = bf16[4,2,4,64,256]{4,1,3,2,0:T(2,128)(2,1)} slice(bf16[4,4,4,64,256]{4,1,3,2,0:T(4,128)(2,1)S(1)} %fusion.4), slice={[0:4:1], [1:4:2], [0:4:1], [0:64:1], [0:256:1]} | slice | bytes 2097152 | tf_op jit(solution)/shard_map/slice | solution.py:118
  209.1 25.4 %slice.320 = bf16[4,2,4,64,256]{4,1,3,2,0:T(2,128)(2,1)} slice(bf16[4,4,4,64,256]{4,1,3,2,0:T(4,128)(2,1)S(1)} %fusion.4), slice={[0:4:1], [0:4:2], [0:4:1], [0:64:1], [0:256:1]} | slice | bytes 2097152 | tf_op jit(solution)/shard_map/slice | solution.py:118
  234.5 3.1 %multiply_convert_fusion = bf16[4,2,4,64,256]{4,1,3,2,0:T(2,128)(2,1)S(1)} fusion(bf16[4,2,4,64,256]{4,1,3,2,0:T(2,128)(2,1)} %slice.321, bf16[4,2,4,64,256]{4,1,3,2,0:T(2,128)(2,1)} %slice.320), kind=kLoop, calls=%fused_computation.44 | loop fusion | flops 2621440 | bytes 3145728 | tf_op jit(solution)/shard_map/convert_element_type | solution.py:119
  237.6 0.9 copy.39
  238.5 0.8 reshape.138
  239.3 1.1 fusion.15
  (99 shorter events, 8.3 us)
Async XLA Ops:
  0.0 239.3 %copy-start = (bf16[1024,256]{1,0:T(8,128)(2,1)S(1)}, bf16[1024,256]{1,0:T(8,128)(2,1)}, u32[]{:S(2)}) copy-start(bf16[1024,256]{1,0:T(8,128)(2,1)} %param.20) | copy-start | bytes 1572868
  4.8 20.5 %all-to-all-start = ((bf16[16,4,3,4,256]{4,3,2,1,0:T(4,128)(2,1)}), bf16[16,4,3,4,256]{4,3,2,1,0:T(4,128)(2,1)S(1)}, u32[]{:S(2)}, u32[]{:S(2)}) async-start(bf16[16,4,3,4,256]{4,3,2,1,0:T(4,128)(2,1)} %reshape.120), calls=%async_computation | async-start | bytes 786432 | tf_op jit(solution)/shard_map/all_to_all | solution.py:176
  25.5 17.2 %copy-start.11 = (bf16[81,128]{1,0:T(8,128)(2,1)S(1)}, bf16[81,128]{1,0:T(8,128)(2,1)}, u32[]{:S(2)}) copy-start(bf16[81,128]{1,0:T(8,128)(2,1)} %param.14) | copy-start | bytes 62212
  25.6 4.9 %collective-permute-start = (bf16[4,2,4,64,3]{3,2,4,1,0:T(4,128)(2,1)S(1)}, bf16[4,2,4,64,3]{3,2,4,1,0:T(4,128)(2,1)S(1)}, u32[]{:S(2)}, u32[]{:S(2)}) collective-permute-start(bf16[4,2,4,64,3]{3,2,4,1,0:T(4,128)(2,1)S(1)} %slice.325), channel_id=1, source_target_pairs={{0,1},{1,2},{2,3},{4,5},{5,6},{6,7},{8,9},{9,10},{10,11},{12,13},{... | collective-permute-start | bytes 36872 | tf_op jit(solution)/shard_map/ppermute | solution.py:14
  30.7 5.9 %collective-permute-start.2 = (bf16[4,6,1,64,3]{3,2,4,1,0:T(2,128)(2,1)S(1)}, bf16[4,6,1,64,3]{3,2,4,1,0:T(2,128)(2,1)S(1)}, u32[]{:S(2)}, u32[]{:S(2)}) collective-permute-start(bf16[4,6,1,64,3]{3,2,4,1,0:T(2,128)(2,1)S(1)} %get-tuple-element.44), channel_id=1, source_target_pairs={{4,0},{8,4},{12,8},{5,1},{9,5},{13,9},{6,2},{10,6},{14,10},{7,3},{... | collective-permute-start | bytes 27656 | tf_op jit(solution)/shard_map/ppermute | solution.py:27
  32.0 6.2 %collective-permute-start.1 = (bf16[4,6,1,64,3]{3,2,4,1,0:T(2,128)(2,1)S(1)}, bf16[4,6,1,64,3]{3,2,4,1,0:T(2,128)(2,1)S(1)}, u32[]{:S(2)}, u32[]{:S(2)}) collective-permute-start(bf16[4,6,1,64,3]{3,2,4,1,0:T(2,128)(2,1)S(1)} %get-tuple-element.43), channel_id=1, source_target_pairs={{0,4},{4,8},{8,12},{1,5},{5,9},{9,13},{2,6},{6,10},{10,14},{3,7},{... | collective-permute-start | bytes 27656 | tf_op jit(solution)/shard_map/ppermute | solution.py:25
  40.3 47.4 %copy-start.14 = (f32[128]{0:T(128)S(1)}, f32[128]{0:T(128)}, u32[]{:S(2)}) copy-start(f32[128]{0:T(128)} %param.15) | copy-start | bytes 1540
  40.3 47.4 %copy-start.15 = (f32[128]{0:T(128)S(1)}, f32[128]{0:T(128)}, u32[]{:S(2)}) copy-start(f32[128]{0:T(128)} %param.16) | copy-start | bytes 1540
  88.4 8.0 %collective-permute-start.3 = (bf16[4,2,4,64,128]{4,3,2,1,0:T(8,128)(2,1)S(1)}, bf16[4,2,4,64,128]{4,3,2,1,0:T(8,128)(2,1)S(1)}, u32[]{:S(2)}, u32[]{:S(2)}) collective-permute-start(bf16[4,2,4,64,128]{4,3,2,1,0:T(8,128)(2,1)S(1)} %slice.357), channel_id=1, source_target_pairs={{0,1},{1,2},{2,3},{4,5},{5,6},{6,7},{8,9},{9,10},{10,11},{12,13},{... | collective-permute-start | bytes 1572872 | tf_op jit(solution)/shard_map/ppermute | solution.py:14
  96.5 9.7 %collective-permute-start.5 = (bf16[4,6,1,64,128]{4,3,2,1,0:T(8,128)(2,1)S(1)}, bf16[4,6,1,64,128]{4,3,2,1,0:T(8,128)(2,1)S(1)}, u32[]{:S(2)}, u32[]{:S(2)}) collective-permute-start(bf16[4,6,1,64,128]{4,3,2,1,0:T(8,128)(2,1)S(1)} %get-tuple-element.40), channel_id=1, source_target_pairs={{4,0},{8,4},{12,8},{5,1},{9,5},{13,9},{6,2},{10,6},{14,10},{7,3},{... | collective-permute-start | bytes 1179656 | tf_op jit(solution)/shard_map/ppermute | solution.py:27
  97.8 9.8 %collective-permute-start.4 = (bf16[4,6,1,64,128]{4,3,2,1,0:T(8,128)(2,1)S(1)}, bf16[4,6,1,64,128]{4,3,2,1,0:T(8,128)(2,1)S(1)}, u32[]{:S(2)}, u32[]{:S(2)}) collective-permute-start(bf16[4,6,1,64,128]{4,3,2,1,0:T(8,128)(2,1)S(1)} %get-tuple-element.39), channel_id=1, source_target_pairs={{0,4},{4,8},{8,12},{1,5},{5,9},{9,13},{2,6},{6,10},{10,14},{3,7},{... | collective-permute-start | bytes 1179656 | tf_op jit(solution)/shard_map/ppermute | solution.py:25
  116.7 1.2 copy-start.1
  116.7 1.5 copy-start.2
  116.7 1.8 copy-start.3
  118.6 1.5 copy-start.8
  124.9 1.3 copy-start.6
  124.9 1.5 copy-start.7
  130.8 1.3 copy-start.4
  130.8 1.5 copy-start.5
  132.4 1.2 copy-start.9
  132.4 1.5 copy-start.10
  135.2 42.1 %copy-start.12 = (f32[256]{0:T(256)S(1)}, f32[256]{0:T(256)}, u32[]{:S(2)}) copy-start(f32[256]{0:T(256)} %param.18) | copy-start | bytes 3076
  135.2 42.2 %copy-start.13 = (f32[256]{0:T(256)S(1)}, f32[256]{0:T(256)}, u32[]{:S(2)}) copy-start(f32[256]{0:T(256)} %param.19) | copy-start | bytes 3076
  234.5 4.8 %copy-start.16 = (f32[256]{0:T(256)S(1)}, f32[256]{0:T(256)}, u32[]{:S(2)}) copy-start(f32[256]{0:T(256)} %param.21) | copy-start | bytes 3076
where the time goes:
time: 241 us; the launch traced here: 240 us
  blocking collectives  80.7 us (33%)
  local copies, waits for them, and re-layouts  71.9 us (30%)
  waiting for transfers between devices  25.7 us (11%)
  starting transfers between devices  25.2 us (10%)
  other arithmetic  20.1 us (8%)
  matrix products  16.2 us (7%)
    psum x2, blocking collectives, norm_silu(): value_sum, square_sum = lax.psum((value_sum, square_sum), ('row', 'tm'))  80.7 us
    slice x1, local copies, waits for them, and re-layouts, encode(): activated[:, 1::2].astype(jnp.float32)  25.5 us
    slice x1, local copies, waits for them, and re-layouts, encode(): activated[:, 0::2].astype(jnp.float32)  25.4 us
    dot_general x9, matrix products, encode(): jnp.dot(tap_strip.reshape(-1, tap_strip.shape[-1]), mixer_weight[time_tap...  13.2 us
    all_to_all x1, waiting for transfers between devices, local(): lax.all_to_all(packed, 'clip', split_axis=0, concat_axis=0, tiled=True)  11.9 us
    ppermute x2, starting transfers between devices, extended_2(): lax.ppermute(tail, axis, [(i, (i + 1) % count) for i in range(ends)])  9.3 us
    all_to_all x1, starting transfers between devices, local(): lax.all_to_all(packed, 'clip', split_axis=0, concat_axis=0, tiled=True)  8.59 us
    slice x3, local copies, waits for them, and re-layouts, encode(): padded[:, time_tap:time_tap + frame_n, row_tap:row_tap + row_n, col_tap:c...  8.15 us
  transfers between devices with their start and end apart: 7, of which 6 were waited for; matrix products, arithmetic and copies ran while one was open for 0% of the time, Pallas kernels for 0%

commit v1 on v0

--- a/solution.py
+++ b/solution.py
@@ -2,6 +2,7 @@
 import jax.numpy as jnp
 from jax import lax
 from jax.sharding import PartitionSpec as P
+from jax.lax import psum
 
 GROUPS = 32
 COLS = 64
@@ -46,7 +47,11 @@
     per_group = chan_n // GROUPS
     value_sum = jnp.sum(hidden, axis=1).reshape(batch_n, GROUPS, per_group).sum(-1)
     square_sum = jnp.sum(hidden * hidden, axis=1).reshape(batch_n, GROUPS, per_group).sum(-1)
-    value_sum, square_sum = lax.psum((value_sum, square_sum), ("row", "tm"))
+
+    def map_row(here_x):
+        return psum(psum(here_x, "tm"), "row")
+
+    value_sum, square_sum = map_row((value_sum, square_sum))
     cell_count = cell_n * per_group * lax.axis_size("row") * lax.axis_size("tm")
     group_mean = value_sum / cell_count
     spread = square_sum / cell_count - group_mean * group_mean

time: 241 us -> 205 us (0.85)
  blocking collectives: 80.7 us -> 43.6 us
    psum x2 -> x4, blocking collectives: 80.7 us -> 43.6 us  [map_row(): return psum(psum(here_x, 'tm'), 'row')]
  transfers between devices with their start and end apart: 7 -> 7, of which waited for: 6 -> 6; matrix products, arithmetic and copies ran while one was open for 0% -> 1% of each run, Pallas kernels for 0% -> 0%
where the time goes in v1:
time: 205 us; the launch traced here: 204 us
  local copies, waits for them, and re-layouts  71.9 us (35%)
  blocking collectives  43.6 us (21%)
  waiting for transfers between devices  25.7 us (13%)
  starting transfers between devices  25.4 us (12%)
  other arithmetic  20.1 us (10%)
  matrix products  16.2 us (8%)
    psum x4, blocking collectives, map_row(): return psum(psum(here_x, 'tm'), 'row')  43.6 us
    slice x1, local copies, waits for them, and re-layouts, encode(): activated[:, 1::2].astype(jnp.float32)  25.5 us
    slice x1, local copies, waits for them, and re-layouts, encode(): activated[:, 0::2].astype(jnp.float32)  25.3 us
    dot_general x9, matrix products, encode(): jnp.dot(tap_strip.reshape(-1, tap_strip.shape[-1]), mixer_weight[time_tap...  13.2 us
    all_to_all x1, waiting for transfers between devices, local(): lax.all_to_all(packed, 'clip', split_axis=0, concat_axis=0, tiled=True)  11.9 us
    ppermute x2, starting transfers between devices, extended_2(): lax.ppermute(tail, axis, [(i, (i + 1) % count) for i in range(ends)])  9.3 us
    all_to_all x1, starting transfers between devices, local(): lax.all_to_all(packed, 'clip', split_axis=0, concat_axis=0, tiled=True)  8.59 us
    slice x3, local copies, waits for them, and re-layouts, encode(): padded[:, time_tap:time_tap + frame_n, row_tap:row_tap + row_n, col_tap:c...  8.19 us
  transfers between devices with their start and end apart: 7, of which 6 were waited for; matrix products, arithmetic and copies ran while one was open for 1% of the time, Pallas kernels for 0%

profile of v1, /device:TPU:32, one launch (start us, length us, event | category | flops | bytes accessed | tf_op | source)
XLA Modules:
  0.0 203.6 jit_solution(6277316989690004933)
XLA Ops:
  0.0 0.9 reshape.119
  1.6 1.3 gather_fusion
  2.9 0.7 compare_select_fusion
  3.8 1.0 reshape.120
  4.8 8.6 %all-to-all-start = ((bf16[16,4,3,4,256]{4,3,2,1,0:T(4,128)(2,1)}), bf16[16,4,3,4,256]{4,3,2,1,0:T(4,128)(2,1)S(1)}, u32[]{:S(2)}, u32[]{:S(2)}) async-start(bf16[16,4,3,4,256]{4,3,2,1,0:T(4,128)(2,1)} %reshape.120), calls=%async_computation | async-start | bytes 786432 | tf_op jit(solution)/shard_map/all_to_all | solution.py:181
  13.4 11.9 %all-to-all-done = bf16[16,4,3,4,256]{4,3,2,1,0:T(4,128)(2,1)S(1)} async-done(((bf16[16,4,3,4,256]{4,3,2,1,0:T(4,128)(2,1)}), bf16[16,4,3,4,256]{4,3,2,1,0:T(4,128)(2,1)S(1)}, u32[]{:S(2)}, u32[]{:S(2)}) %all-to-all-start) | async-done | bytes 393248 | tf_op jit(solution)/shard_map/all_to_all | solution.py:181
  25.6 3.4 %collective-permute-start = (bf16[4,2,4,64,3]{3,2,4,1,0:T(4,128)(2,1)S(1)}, bf16[4,2,4,64,3]{3,2,4,1,0:T(4,128)(2,1)S(1)}, u32[]{:S(2)}, u32[]{:S(2)}) collective-permute-start(bf16[4,2,4,64,3]{3,2,4,1,0:T(4,128)(2,1)S(1)} %slice.325), channel_id=1, source_target_pairs={{0,1},{1,2},{2,3},{4,5},{5,6},{6,7},{8,9},{9,10},{10,11},{12,13},{... | collective-permute-start | bytes 36872 | tf_op jit(solution)/shard_map/ppermute | solution.py:15
  29.0 1.5 collective-permute-done
  30.7 1.3 collective-permute-start.2
  32.0 4.5 %collective-permute-start.1 = (bf16[4,6,1,64,3]{3,2,4,1,0:T(2,128)(2,1)S(1)}, bf16[4,6,1,64,3]{3,2,4,1,0:T(2,128)(2,1)S(1)}, u32[]{:S(2)}, u32[]{:S(2)}) collective-permute-start(bf16[4,6,1,64,3]{3,2,4,1,0:T(2,128)(2,1)S(1)} %get-tuple-element.47), channel_id=1, source_target_pairs={{0,4},{4,8},{8,12},{1,5},{5,9},{9,13},{2,6},{6,10},{10,14},{3,7},{... | collective-permute-start | bytes 27656 | tf_op jit(solution)/shard_map/ppermute | solution.py:26
  36.5 1.6 collective-permute-done.1
  40.5 2.1 %copy.36 = bf16[4,4,4,64,81]{4,3,2,1,0:T(8,128)(2,1)} copy(bf16[4,4,4,64,81]{3,2,4,1,0:T(4,128)(2,1)S(1)} %constant_dynamic-update-slice_fusion) | data formatting | bytes 1327104 | tf_op jit(solution)/shard_map/concatenate | solution.py:92
  42.7 1.6 fusion.49
  44.7 11.3 %all-reduce.3 = (f32[4,32]{1,0:T(4,128)S(1)}, f32[4,32]{1,0:T(4,128)S(1)}) all-reduce(f32[4,32]{1,0:T(4,128)S(1)} %reduce_sum.88, f32[4,32]{1,0:T(4,128)S(1)} %reduce_sum.86), channel_id=1, replica_groups=mesh['clip'=16,'row'=4,'tm'=4] {'tm'}, use_global_device_ids=true, to_apply=%region_7.8 | all-reduce | flops 256 | bytes 2048 | tf_op jit(solution)/shard_map/psum | solution.py:52
  56.0 11.8 %all-reduce.5 = (f32[4,32]{1,0:T(4,128)S(1)}, f32[4,32]{1,0:T(4,128)S(1)}) all-reduce(f32[4,32]{1,0:T(4,128)S(1)} %get-tuple-element.11, f32[4,32]{1,0:T(4,128)S(1)} %get-tuple-element.12), channel_id=1, replica_groups=mesh['clip'=16,'row'=4,'tm'=4] {'row'}, use_global_device_ids=true, to_apply=%region_8.9 | all-reduce | flops 256 | bytes 2048 | tf_op jit(solution)/shard_map/psum | solution.py:52
  68.9 1.6 collective-permute-start.3
  70.5 6.6 %collective-permute-done.3 = bf16[4,2,4,64,128]{4,3,2,1,0:T(8,128)(2,1)S(1)} collective-permute-done((bf16[4,2,4,64,128]{4,3,2,1,0:T(8,128)(2,1)S(1)}, bf16[4,2,4,64,128]{4,3,2,1,0:T(8,128)(2,1)S(1)}, u32[]{:S(2)}, u32[]{:S(2)}) %collective-permute-start.3) | collective-permute-done | bytes 524320 | tf_op jit(solution)/shard_map/ppermute | solution.py:15
  77.3 1.3 collective-permute-start.5
  78.6 4.8 %collective-permute-start.4 = (bf16[4,6,1,64,128]{4,3,2,1,0:T(8,128)(2,1)S(1)}, bf16[4,6,1,64,128]{4,3,2,1,0:T(8,128)(2,1)S(1)}, u32[]{:S(2)}, u32[]{:S(2)}) collective-permute-start(bf16[4,6,1,64,128]{4,3,2,1,0:T(8,128)(2,1)S(1)} %get-tuple-element.43), channel_id=1, source_target_pairs={{0,4},{4,8},{8,12},{1,5},{5,9},{9,13},{2,6},{6,10},{10,14},{3,7},{... | collective-permute-start | bytes 1179656 | tf_op jit(solution)/shard_map/ppermute | solution.py:26
  83.3 1.1 fusion.16
  84.4 2.6 %collective-permute-done.5 = bf16[4,6,1,64,128]{4,3,2,1,0:T(8,128)(2,1)S(1)} collective-permute-done((bf16[4,6,1,64,128]{4,3,2,1,0:T(8,128)(2,1)S(1)}, bf16[4,6,1,64,128]{4,3,2,1,0:T(8,128)(2,1)S(1)}, u32[]{:S(2)}, u32[]{:S(2)}) %collective-permute-start.5) | collective-permute-done | bytes 393248 | tf_op jit(solution)/shard_map/ppermute | solution.py:28
  86.9 1.5 collective-permute-done.4
  88.4 1.4 select_maximum_fusion
  89.8 6.3 %fusion.50 = (bf16[4,4,4,64,128]{4,3,2,1,0:T(8,128)(2,1)}, bf16[4,4,4,64,128]{4,3,2,1,0:T(8,128)(2,1)}, bf16[4,4,4,64,128]{4,3,2,1,0:T(8,128)(2,1)}, bf16[4,4,4,...) fusion(bf16[4,6,6,66,128]{4,3,2,1,0:T(8,128)(2,1)S(1)} %select_, ...), kind=kLoop, calls=%fused_computation.143 | loop fusion | bytes 37748736 | tf_op jit(solution)/shard_map/slice | solution.py:103
  96.6 0.9 fusion.52
  97.6 1.0 fusion.51
  99.4 1.1 pad_maximum_fusion.1
  100.9 1.2 fusion.28
  102.1 1.2 convolution_add_fusion.7
  103.4 1.1 pad_maximum_fusion.3
  104.4 1.2 convolution_add_fusion.6
  105.7 1.2 convolution_add_fusion.5
  107.8 1.2 convolution_add_fusion.4
  109.0 1.3 pad_maximum_fusion.5
  110.4 1.3 convolution_add_fusion.3
  111.7 1.2 convolution_add_fusion.2
  113.7 0.7 copy-done.9
  114.7 1.3 convolution_add_fusion.1
  116.0 3.2 %bitcast_reduce_fusion = (f32[4,256]{1,0:T(4,128)S(1)}, f32[4,256]{1,0:T(4,128)S(1)}, f32[4096,256]{1,0:T(8,128)}) fusion(f32[4096,256]{1,0:T(8,128)S(1)} %convolution_add_fusion.1, bf16[4096,384]{1,0:T(8,128)(2,1)S(1)} %bitcast.87, bf16[3,3,384,256]{3,2,1,0:T(8,128)(2,1)S(1)} %copy-done.8), kind=kOutput, calls=%fused_computation.14 | convolution fusion | flops 809498624 | bytes 11739136 | tf_op jit(solution)/shard_map/dot_general | solution.py:113
  119.6 10.3 %all-reduce.2 = (f32[4,32]{1,0:T(4,128)S(1)}, f32[4,32]{1,0:T(4,128)S(1)}) all-reduce(f32[4,32]{1,0:T(4,128)S(1)} %reduce_sum.92, f32[4,32]{1,0:T(4,128)S(1)} %reduce_sum.90), channel_id=1, replica_groups=mesh['clip'=16,'row'=4,'tm'=4] {'tm'}, use_global_device_ids=true, to_apply=%region_15.16 | all-reduce | flops 256 | bytes 2048 | tf_op jit(solution)/shard_map/psum | solution.py:52
  129.9 10.2 %all-reduce.4 = (f32[4,32]{1,0:T(4,128)S(1)}, f32[4,32]{1,0:T(4,128)S(1)}) all-reduce(f32[4,32]{1,0:T(4,128)S(1)} %get-tuple-element.9, f32[4,32]{1,0:T(4,128)S(1)} %get-tuple-element.10), channel_id=1, replica_groups=mesh['clip'=16,'row'=4,'tm'=4] {'row'}, use_global_device_ids=true, to_apply=%region_16.17 | all-reduce | flops 256 | bytes 2048 | tf_op jit(solution)/shard_map/psum | solution.py:52
  140.6 6.2 %fusion.4 = bf16[4,4,4,64,256]{4,1,3,2,0:T(4,128)(2,1)S(1)} fusion(f32[4,4,4,64,256]{4,3,2,1,0:T(8,128)} %bitcast.86, f32[256]{0:T(256)S(1)} %copy-done.13, f32[4,256]{1,0:T(4,128)S(1)} %broadcast_multiply_fusion, f32[4,256]{1,0:T(4,128)S(1)} %sub.31), kind=kLoop, calls=%fused_computation.19 | loop fusion | flops 8388608 | bytes 6300672 | tf_op jit(solution)/shard_map/convert_element_type | solution.py:118
  146.8 25.5 %slice.321 = bf16[4,2,4,64,256]{4,1,3,2,0:T(2,128)(2,1)} slice(bf16[4,4,4,64,256]{4,1,3,2,0:T(4,128)(2,1)S(1)} %fusion.4), slice={[0:4:1], [1:4:2], [0:4:1], [0:64:1], [0:256:1]} | slice | bytes 2097152 | tf_op jit(solution)/shard_map/slice | solution.py:123
  172.3 25.3 %slice.320 = bf16[4,2,4,64,256]{4,1,3,2,0:T(2,128)(2,1)} slice(bf16[4,4,4,64,256]{4,1,3,2,0:T(4,128)(2,1)S(1)} %fusion.4), slice={[0:4:1], [0:4:2], [0:4:1], [0:64:1], [0:256:1]} | slice | bytes 2097152 | tf_op jit(solution)/shard_map/slice | solution.py:123
  197.6 3.1 %multiply_convert_fusion = bf16[4,2,4,64,256]{4,1,3,2,0:T(2,128)(2,1)S(1)} fusion(bf16[4,2,4,64,256]{4,1,3,2,0:T(2,128)(2,1)} %slice.321, bf16[4,2,4,64,256]{4,1,3,2,0:T(2,128)(2,1)} %slice.320), kind=kLoop, calls=%fused_computation.44 | loop fusion | flops 2621440 | bytes 3145728 | tf_op jit(solution)/shard_map/convert_element_type | solution.py:124
  200.8 0.9 copy.39
  201.6 0.8 reshape.138
  202.4 1.1 fusion.15
  (101 shorter events, 9.6 us)
Async XLA Ops:
  0.0 202.4 %copy-start = (bf16[1024,256]{1,0:T(8,128)(2,1)S(1)}, bf16[1024,256]{1,0:T(8,128)(2,1)}, u32[]{:S(2)}) copy-start(bf16[1024,256]{1,0:T(8,128)(2,1)} %param.20) | copy-start | bytes 1572868
  4.8 20.5 %all-to-all-start = ((bf16[16,4,3,4,256]{4,3,2,1,0:T(4,128)(2,1)}), bf16[16,4,3,4,256]{4,3,2,1,0:T(4,128)(2,1)S(1)}, u32[]{:S(2)}, u32[]{:S(2)}) async-start(bf16[16,4,3,4,256]{4,3,2,1,0:T(4,128)(2,1)} %reshape.120), calls=%async_computation | async-start | bytes 786432 | tf_op jit(solution)/shard_map/all_to_all | solution.py:181
  25.5 17.2 %copy-start.11 = (bf16[81,128]{1,0:T(8,128)(2,1)S(1)}, bf16[81,128]{1,0:T(8,128)(2,1)}, u32[]{:S(2)}) copy-start(bf16[81,128]{1,0:T(8,128)(2,1)} %param.14) | copy-start | bytes 62212
  25.6 4.9 %collective-permute-start = (bf16[4,2,4,64,3]{3,2,4,1,0:T(4,128)(2,1)S(1)}, bf16[4,2,4,64,3]{3,2,4,1,0:T(4,128)(2,1)S(1)}, u32[]{:S(2)}, u32[]{:S(2)}) collective-permute-start(bf16[4,2,4,64,3]{3,2,4,1,0:T(4,128)(2,1)S(1)} %slice.325), channel_id=1, source_target_pairs={{0,1},{1,2},{2,3},{4,5},{5,6},{6,7},{8,9},{9,10},{10,11},{12,13},{... | collective-permute-start | bytes 36872 | tf_op jit(solution)/shard_map/ppermute | solution.py:15
  30.7 5.9 %collective-permute-start.2 = (bf16[4,6,1,64,3]{3,2,4,1,0:T(2,128)(2,1)S(1)}, bf16[4,6,1,64,3]{3,2,4,1,0:T(2,128)(2,1)S(1)}, u32[]{:S(2)}, u32[]{:S(2)}) collective-permute-start(bf16[4,6,1,64,3]{3,2,4,1,0:T(2,128)(2,1)S(1)} %get-tuple-element.48), channel_id=1, source_target_pairs={{4,0},{8,4},{12,8},{5,1},{9,5},{13,9},{6,2},{10,6},{14,10},{7,3},{... | collective-permute-start | bytes 27656 | tf_op jit(solution)/shard_map/ppermute | solution.py:28
  32.0 6.2 %collective-permute-start.1 = (bf16[4,6,1,64,3]{3,2,4,1,0:T(2,128)(2,1)S(1)}, bf16[4,6,1,64,3]{3,2,4,1,0:T(2,128)(2,1)S(1)}, u32[]{:S(2)}, u32[]{:S(2)}) collective-permute-start(bf16[4,6,1,64,3]{3,2,4,1,0:T(2,128)(2,1)S(1)} %get-tuple-element.47), channel_id=1, source_target_pairs={{0,4},{4,8},{8,12},{1,5},{5,9},{9,13},{2,6},{6,10},{10,14},{3,7},{... | collective-permute-start | bytes 27656 | tf_op jit(solution)/shard_map/ppermute | solution.py:26
  40.3 27.9 %copy-start.14 = (f32[128]{0:T(128)S(1)}, f32[128]{0:T(128)}, u32[]{:S(2)}) copy-start(f32[128]{0:T(128)} %param.15) | copy-start | bytes 1540
  40.3 27.9 %copy-start.15 = (f32[128]{0:T(128)S(1)}, f32[128]{0:T(128)}, u32[]{:S(2)}) copy-start(f32[128]{0:T(128)} %param.16) | copy-start | bytes 1540
  68.9 8.2 %collective-permute-start.3 = (bf16[4,2,4,64,128]{4,3,2,1,0:T(8,128)(2,1)S(1)}, bf16[4,2,4,64,128]{4,3,2,1,0:T(8,128)(2,1)S(1)}, u32[]{:S(2)}, u32[]{:S(2)}) collective-permute-start(bf16[4,2,4,64,128]{4,3,2,1,0:T(8,128)(2,1)S(1)} %slice.357), channel_id=1, source_target_pairs={{0,1},{1,2},{2,3},{4,5},{5,6},{6,7},{8,9},{9,10},{10,11},{12,13},{... | collective-permute-start | bytes 1572872 | tf_op jit(solution)/shard_map/ppermute | solution.py:15
  77.3 9.7 %collective-permute-start.5 = (bf16[4,6,1,64,128]{4,3,2,1,0:T(8,128)(2,1)S(1)}, bf16[4,6,1,64,128]{4,3,2,1,0:T(8,128)(2,1)S(1)}, u32[]{:S(2)}, u32[]{:S(2)}) collective-permute-start(bf16[4,6,1,64,128]{4,3,2,1,0:T(8,128)(2,1)S(1)} %get-tuple-element.44), channel_id=1, source_target_pairs={{4,0},{8,4},{12,8},{5,1},{9,5},{13,9},{6,2},{10,6},{14,10},{7,3},{... | collective-permute-start | bytes 1179656 | tf_op jit(solution)/shard_map/ppermute | solution.py:28
  78.6 9.8 %collective-permute-start.4 = (bf16[4,6,1,64,128]{4,3,2,1,0:T(8,128)(2,1)S(1)}, bf16[4,6,1,64,128]{4,3,2,1,0:T(8,128)(2,1)S(1)}, u32[]{:S(2)}, u32[]{:S(2)}) collective-permute-start(bf16[4,6,1,64,128]{4,3,2,1,0:T(8,128)(2,1)S(1)} %get-tuple-element.43), channel_id=1, source_target_pairs={{0,4},{4,8},{8,12},{1,5},{5,9},{9,13},{2,6},{6,10},{10,14},{3,7},{... | collective-permute-start | bytes 1179656 | tf_op jit(solution)/shard_map/ppermute | solution.py:26
  97.5 1.2 copy-start.1
  97.5 1.5 copy-start.2
  97.5 1.8 copy-start.3
  99.4 1.5 copy-start.8
  105.7 1.3 copy-start.6
  105.7 1.5 copy-start.7
  111.6 1.3 copy-start.4
  111.7 1.5 copy-start.5
  113.2 1.2 copy-start.9
  113.2 1.5 copy-start.10
  116.0 24.5 %copy-start.12 = (f32[256]{0:T(256)S(1)}, f32[256]{0:T(256)}, u32[]{:S(2)}) copy-start(f32[256]{0:T(256)} %param.18) | copy-start | bytes 3076
  116.0 24.6 %copy-start.13 = (f32[256]{0:T(256)S(1)}, f32[256]{0:T(256)}, u32[]{:S(2)}) copy-start(f32[256]{0:T(256)} %param.19) | copy-start | bytes 3076
  197.6 4.8 %copy-start.16 = (f32[256]{0:T(256)S(1)}, f32[256]{0:T(256)}, u32[]{:S(2)}) copy-start(f32[256]{0:T(256)} %param.21) | copy-start | bytes 3076
